TPU v7x, 32 devices: a whole 2x2x4 slice. The times are simulated.
32 devices in a mesh: row: 4 (over y, core), col: 8 (over z, x).
Axes of the slice: x: 2, y: 2, z: 4, core: 2. Of those that a mesh axis runs over, the one named last changes fastest.
Arguments:
- ancestor_inverse: float32 [12288, 12288], P('row', 'col')
- factor: bfloat16 [3, 12288, 512], P(None, ('row', 'col')), may hold values from -0.5 to 0.5
- coupling: float32 [3, 512, 512], replicated, may hold values from -0.25 to 0.25
- diagonal_inverse: float32 [3, 512, 512], replicated, may hold values from -6 to 6
- ancestors: int32 [3, 24], replicated, may hold values from -1 to 23, as said below
Outputs:
- block_columns: float32 [3, 12288, 512], P(None, ('row', 'col'))
- block_rows: float32 [3, 12288, 512], P(None, ('col', 'row'))
- node_blocks: float32 [3, 3, 512, 512], replicated
Inputs may be any that keep to these rules, and one draw needn't show every extreme that they name: `ancestors`: row k lists the ancestor block rows of supernode k, blocks of 512 rows: distinct indices in increasing order, then -1 in the slots left. Every block is listed by some supernode.
All inputs are finite; a program needn't handle non-finite values.
Results may differ from a plain program's by a relative error of at most 0.0003.
Values may be sent and summed in bfloat16 or wider, within the bound.
No kernel may reach another device: no remote copies, remote signals or barrier semaphores. Data moves between devices by JAX's collectives and lax.ppermute only.
A program may use at most 128 MiB of HBM per device.

v0:
```python
import jax
import jax.numpy as jnp
from jax import lax
from jax.sharding import PartitionSpec as P

highest = lax.Precision.HIGHEST


def broadcast(value, axis, source):
    kept = jnp.where(lax.axis_index(axis) == source, value, 0).astype(value.dtype)
    return lax.psum(kept, axis)


def matmul(left, right):
    return jnp.dot(left, right, precision=highest)


def left_dot(left, right):
    return lax.dot_general(left, right, (((0,), (0,)), ((), ())), precision=highest)


def pair_index(later, earlier):
    return later * (later - 1) // 2 + earlier


def local(ancestor_inverse, factor, coupling, diagonal_inverse, ancestors):
    col_count = lax.axis_size("col")
    row_index = lax.axis_index("row")
    col_index = lax.axis_index("col")
    nodes_total, piece_rows, sn_width = factor.shape
    rows_here, cols_here = ancestor_inverse.shape
    group_ratio = rows_here // cols_here
    first_row = (row_index * col_count + col_index) * piece_rows
    block_of_row = (first_row + jnp.arange(piece_rows, dtype=jnp.int32)) // sn_width
    source_row = col_index // group_ratio
    block_start = col_index % group_ratio * cols_here
    row_layout = []
    col_layout = []
    solved = {}
    for current in range(nodes_total):
        listed = jnp.any(ancestors[current][:, None] == block_of_row[None, :], axis=0)
        lower_part = jnp.where(listed[:, None], factor[current], jnp.zeros_like(factor[current]))
        lower_rows = lax.all_gather(lower_part, "col", axis=0, tiled=True)
        own_block = lax.dynamic_slice_in_dim(lower_rows, block_start, cols_here, 0)
        lower_cols = broadcast(own_block, "row", source_row).astype(jnp.float32)
        lower_here = lower_part.astype(jnp.float32)
        product_sum = lax.psum_scatter(
            matmul(ancestor_inverse, lower_cols), "col", scatter_dimension=0, tiled=True
        )
        for earlier in range(current):
            product_sum = product_sum + matmul(
                row_layout[earlier], coupling[pair_index(current, earlier)]
            )
        column = -product_sum
        stacked = jnp.concatenate(row_layout + [column], axis=1)
        summed = lax.psum(left_dot(lower_here, stacked), ("row", "col"))
        crosses = [
            summed[:, earlier * sn_width : (earlier + 1) * sn_width] for earlier in range(current)
        ]
        self_term = summed[:, current * sn_width : (current + 1) * sn_width]
        for earlier in range(current):
            block_value = -crosses[earlier].T
            for inner in range(current):
                block_value = block_value - matmul(
                    solved[earlier, inner], coupling[pair_index(current, inner)]
                )
            solved[earlier, current] = block_value
            solved[current, earlier] = block_value.T
        diag_value = diagonal_inverse[current] - self_term
        for earlier in range(current):
            diag_value = diag_value - left_dot(
                coupling[pair_index(current, earlier)], solved[earlier, current]
            )
        solved[current, current] = diag_value
        rows_float = lower_rows.astype(jnp.float32)
        mirror = lax.psum_scatter(
            left_dot(ancestor_inverse, rows_float), "row", scatter_dimension=0, tiled=True
        )
        for earlier in range(current):
            mirror = mirror + matmul(col_layout[earlier], coupling[pair_index(current, earlier)])
        col_layout.append(-mirror)
        row_layout.append(column)
    finished = jnp.stack(row_layout)
    mirrored_all = jnp.stack(col_layout)
    node_blocks = jnp.stack(
        [
            jnp.stack([solved[first_node, second_node] for second_node in range(nodes_total)])
            for first_node in range(nodes_total)
        ]
    )
    return (finished, mirrored_all, node_blocks)


def solution(mesh):
    placed = (P("row", "col"), P(None, ("row", "col"), None), P(), P(), P())
    return jax.shard_map(
        local,
        mesh=mesh,
        in_specs=placed,
        out_specs=(P(None, ("row", "col"), None), P(None, ("col", "row"), None), P()),
        check_vma=False,
    )
```

profile of v0, /device:TPU:0, one launch (start us, length us, event | category | flops | bytes accessed | tf_op | source)
XLA Modules:
  0.0 1007.5 jit_solution(5974017174490358877)
XLA Ops:
  7.2 0.8 slice_bitcast_fusion.2
  8.1 2.5 bitcast_select_fusion.1
  10.7 0.7 all-gather.4.cloned.1.call-update
  11.5 0.7 all-gather.6.cloned.1.call-update
  12.2 61.3 %all-gather.8.cloned.1.call-done = bf16[3072,512]{1,0:T(8,128)(2,1)} async-done(((bf16[384,512]{1,0:T(8,128)(2,1)}), bf16[3072,512]{1,0:T(8,128)(2,1)}) %all-gather.8.cloned.1.call-update) | async-done | bytes 3145744 | tf_op jit(solution)/shard_map/all_gather | solution.py:43
  73.6 2.8 dynamic-slice_select_fusion
  76.4 58.1 %all-gather.4.cloned.1.call-done = bf16[3072,512]{1,0:T(8,128)(2,1)} async-done(((bf16[384,512]{1,0:T(8,128)(2,1)}), bf16[3072,512]{1,0:T(8,128)(2,1)}) %all-gather.4.cloned.1.call-update) | async-done | bytes 3145744 | tf_op jit(solution)/shard_map/all_gather | solution.py:43
  134.5 2.8 dynamic-slice_select_fusion.2
  137.3 58.1 %all-gather.6.cloned.1.call-done = bf16[3072,512]{1,0:T(8,128)(2,1)} async-done(((bf16[384,512]{1,0:T(8,128)(2,1)}), bf16[3072,512]{1,0:T(8,128)(2,1)}) %all-gather.6.cloned.1.call-update) | async-done | bytes 3145744 | tf_op jit(solution)/shard_map/all_gather | solution.py:43
  195.4 2.8 dynamic-slice_select_fusion.1
  198.3 92.8 %all-reduce.7.cloned.1.call-done = (bf16[1536,512]{1,0:T(8,128)(2,1)}, bf16[1536,512]{1,0:T(8,128)(2,1)}, bf16[1536,512]{1,0:T(8,128)(2,1)}) async-done(((bf16[1536,512]{1,0:T(8,128)(2,1)}, bf16[1536,512]{1,0:T(8,128)(2,1)}, bf16[1536,512]{1,0:T(8,128)(2,1)}), (bf16[1536,512]{1,0:T(8,128)(2,1)}, bf16[1536,512]{1,0:T(8,128)(2,1)}, bf16[1536,512]{1,0:T(8,128)(2,1)})) %all-reduce.7.cloned.1.call-update) | async-done | bytes 4718608 | tf_op jit(solution)/shard_map/psum | solution.py:11
  291.1 22.4 %convolution_bitcast_fusion.2 = f32[3072,512]{0,1:T(8,128)} fusion(bf16[1536,512]{1,0:T(8,128)(2,1)} %get-tuple-element.16, f32[3072,1536]{1,0:T(8,128)} %param.5), kind=kOutput, calls=%fused_computation.3 | convolution fusion | flops 28991029248 | bytes 26738688 | tf_op jit(solution)/shard_map/dot_general | solution.py:15
  313.5 1.3 copy-done.30
  314.9 21.8 %convolution_bitcast_fusion.1 = f32[3072,512]{0,1:T(8,128)} fusion(bf16[1536,512]{1,0:T(8,128)(2,1)S(1)} %copy-done.30, f32[3072,1536]{1,0:T(8,128)} %param.5), kind=kOutput, calls=%fused_computation.2 | convolution fusion | flops 28991029248 | bytes 26738688 | tf_op jit(solution)/shard_map/dot_general | solution.py:15
  336.7 0.5 reduce-scatter.11.cloned.1.call-start
  337.2 0.9 copy-done.29
  338.1 21.8 %convolution_bitcast_fusion = f32[3072,512]{0,1:T(8,128)} fusion(bf16[1536,512]{1,0:T(8,128)(2,1)S(1)} %copy-done.29, f32[3072,1536]{1,0:T(8,128)} %param.5), kind=kOutput, calls=%fused_computation.1 | convolution fusion | flops 28991029248 | bytes 26738688 | tf_op jit(solution)/shard_map/dot_general | solution.py:15
  360.0 1.9 copy-done.28
  361.8 19.7 %convolution_bitcast_fusion.3 = f32[1536,512]{0,1:T(8,128)} fusion(bf16[3072,512]{1,0:T(8,128)(2,1)S(1)} %copy-done.28, f32[3072,1536]{1,0:T(8,128)} %param.5), kind=kOutput, calls=%fused_computation.4 | convolution fusion | flops 28991029248 | bytes 25165824 | tf_op jit(solution)/shard_map/dot_general | solution.py:19
  381.8 1.7 copy-done.27
  383.5 19.9 %convolution_bitcast_fusion.5 = f32[1536,512]{0,1:T(8,128)} fusion(bf16[3072,512]{1,0:T(8,128)(2,1)S(1)} %copy-done.27, f32[3072,1536]{1,0:T(8,128)} %param.5), kind=kOutput, calls=%fused_computation.6 | convolution fusion | flops 28991029248 | bytes 25165824 | tf_op jit(solution)/shard_map/dot_general | solution.py:19
  403.5 1.8 copy-done.26
  405.3 19.7 %convolution_bitcast_fusion.4 = f32[1536,512]{0,1:T(8,128)} fusion(bf16[3072,512]{1,0:T(8,128)(2,1)S(1)} %copy-done.26, f32[3072,1536]{1,0:T(8,128)} %param.5), kind=kOutput, calls=%fused_computation.5 | convolution fusion | flops 28991029248 | bytes 25165824 | tf_op jit(solution)/shard_map/dot_general | solution.py:19
  425.3 6.5 reduce-scatter.7.cloned.1.call-done
  431.8 2.4 fusion.73
  434.2 3.3 fusion.64
  437.5 115.1 %reduce-scatter.9.cloned.1.call-done = f32[384,512]{0,1:T(8,128)} async-done(((f32[3072,512]{0,1:T(8,128)}), f32[384,512]{0,1:T(8,128)}) %reduce-scatter.9.cloned.1.call-update) | async-done | bytes 786448 | tf_op jit(solution)/shard_map/reduce_scatter | solution.py:47
  552.6 3.4 fusion.14
  555.9 0.9 copy-done.3
  556.9 3.1 fusion.6
  560.0 114.0 %reduce-scatter.11.cloned.1.call-done = f32[384,512]{0,1:T(8,128)} async-done(((f32[3072,512]{0,1:T(8,128)}), f32[384,512]{0,1:T(8,128)}) %reduce-scatter.11.cloned.1.call-update) | async-done | bytes 786448 | tf_op jit(solution)/shard_map/reduce_scatter | solution.py:47
  674.0 3.3 convolution_add_fusion.4
  677.4 1.9 fusion.15
  679.3 0.9 copy-done.12
  680.2 4.5 fusion
  684.7 2.3 slice.74
  687.0 2.9 copy.65
  690.0 23.6 %reduce-scatter.17.cloned.1.call-done = f32[384,512]{0,1:T(8,128)} async-done(((f32[1536,512]{0,1:T(8,128)}), f32[384,512]{0,1:T(8,128)}) %reduce-scatter.17.cloned.1.call-update) | async-done | bytes 786448 | tf_op jit(solution)/shard_map/reduce_scatter | solution.py:76
  713.6 40.3 %reduce-scatter.13.cloned.1.call-done = f32[384,512]{0,1:T(8,128)} async-done(((f32[1536,512]{0,1:T(8,128)}), f32[384,512]{0,1:T(8,128)}) %reduce-scatter.13.cloned.1.call-update) | async-done | bytes 786448 | tf_op jit(solution)/shard_map/reduce_scatter | solution.py:76
  753.9 4.1 convolution_add_fusion.1
  758.0 36.0 %reduce-scatter.15.cloned.1.call-done = f32[384,512]{0,1:T(8,128)} async-done(((f32[1536,512]{0,1:T(8,128)}), f32[384,512]{0,1:T(8,128)}) %reduce-scatter.15.cloned.1.call-update) | async-done | bytes 786448 | tf_op jit(solution)/shard_map/reduce_scatter | solution.py:76
  794.0 3.4 fusion.16
  797.4 1.9 fusion.18
  799.4 1.6 pad_maximum_fusion.2
  800.9 3.0 copy.51
  804.0 3.2 pad_maximum_fusion.1
  807.1 3.2 copy.50
  810.3 146.5 %all-reduce.5.cloned.1.call-done = (f32[512,1536]{1,0:T(8,128)}, f32[512,512]{1,0:T(8,128)}, f32[512,1024]{0,1:T(8,128)}) async-done(((f32[512,1536]{1,0:T(8,128)}, f32[512,512]{1,0:T(8,128)}, f32[512,1024]{0,1:T(8,128)}), (f32[512,1536]{1,0:T(8,128)}, f32[512,512]{1,0:T(8,128)}, f32[512,1024]{0,1:T(8,128)})) %all-reduce.5.cloned.1.call-update) | async-done | bytes 6291472 | tf_op jit(solution)/shard_map/psum | solution.py:56
  956.9 3.6 fusion.34
  960.5 3.2 bitcast_subtract_fusion.7
  963.7 1.9 fusion.32
  965.6 1.9 fusion.27
  967.5 2.0 fusion.13
  969.5 1.0 copy-done.8
  970.5 1.9 fusion.25
  972.4 3.3 fusion.12
  975.7 2.3 fusion.20
  978.0 2.3 fusion.70
  980.3 2.5 copy.39
  982.9 5.3 fusion.11
  988.2 2.0 maximum_bitcast_fusion.1
  990.1 2.4 copy.49
  992.6 2.3 maximum_bitcast_fusion.2
  995.6 5.1 pad_maximum_fusion
  (77 shorter events, 1.9 us)
Async XLA Ops:
  7.2 66.4 %all-gather.8.cloned.1.call-start = ((), (), s32[]{:S(2)}) async-start(), calls=%async_computation.10 | async-start | bytes 3538944 | tf_op jit(solution)/shard_map/all_gather | solution.py:43
  10.7 123.8 %all-gather.4.cloned.1.call-start = ((), (), s32[]{:S(2)}) async-start(), calls=%async_computation.6 | async-start | bytes 3538944 | tf_op jit(solution)/shard_map/all_gather | solution.py:43
  11.4 183.9 %all-gather.6.cloned.1.call-start = ((), (), s32[]{:S(2)}) async-start(), calls=%async_computation.8 | async-start | bytes 3538944 | tf_op jit(solution)/shard_map/all_gather | solution.py:43
  12.2 278.9 %all-reduce.7.cloned.1.call-start = ((), (), s32[]{:S(2)}) async-start(), calls=%async_computation.16 | async-start | bytes 9437184 | tf_op jit(solution)/shard_map/psum | solution.py:11
  198.2 233.6 %reduce-scatter.7.cloned.1.call-start = ((), (), s32[]{:S(2)}) async-start(), calls=%async_computation.7 | async-start | bytes 7077888 | tf_op jit(solution)/shard_map/reduce_scatter | solution.py:47
  313.5 1.4 copy-start.30
  313.5 239.1 %reduce-scatter.9.cloned.1.call-start = ((), (), s32[]{:S(2)}) async-start(), calls=%async_computation.9 | async-start | bytes 7077888 | tf_op jit(solution)/shard_map/reduce_scatter | solution.py:47
  336.7 1.4 copy-start.29
  336.7 337.3 %reduce-scatter.11.cloned.1.call-start = ((), (), s32[]{:S(2)}) async-start(), calls=%async_computation.11 | async-start | bytes 7077888 | tf_op jit(solution)/shard_map/reduce_scatter | solution.py:47
  359.9 1.9 copy-start.28
  359.9 353.6 %reduce-scatter.17.cloned.1.call-start = ((), (), s32[]{:S(2)}) async-start(), calls=%async_computation.14 | async-start | bytes 3932160 | tf_op jit(solution)/shard_map/reduce_scatter | solution.py:76
  381.6 2.0 copy-start.27
  381.6 372.2 %reduce-scatter.13.cloned.1.call-start = ((), (), s32[]{:S(2)}) async-start(), calls=%async_computation.12 | async-start | bytes 3932160 | tf_op jit(solution)/shard_map/reduce_scatter | solution.py:76
  403.4 1.9 copy-start.26
  403.5 390.5 %reduce-scatter.15.cloned.1.call-start = ((), (), s32[]{:S(2)}) async-start(), calls=%async_computation.13 | async-start | bytes 3932160 | tf_op jit(solution)/shard_map/reduce_scatter | solution.py:76
  425.0 9.2 copy-start.23
  425.0 127.6 %copy-start = (f32[3,512,512]{2,1,0:T(8,128)S(1)}, f32[3,512,512]{2,1,0:T(8,128)}, u32[]{:S(2)}) copy-start(f32[3,512,512]{2,1,0:T(8,128)} %param.7) | copy-start | bytes 9437188
  425.0 531.9 %all-reduce.5.cloned.1.call-start = ((), (), s32[]{:S(2)}) async-start(), calls=%async_computation.15 | async-start | bytes 12582912 | tf_op jit(solution)/shard_map/psum | solution.py:56
  437.5 119.4 %copy-start.24 = (bf16[384,512]{1,0:T(8,128)(2,1)S(1)}, bf16[384,512]{1,0:T(8,128)(2,1)}, u32[]{:S(2)}) copy-start(bf16[384,512]{1,0:T(8,128)(2,1)} %get-tuple-element.22) | copy-start | bytes 1179652
  552.6 4.3 copy-start.13
  555.9 0.9 copy-start.3
  560.0 120.2 %copy-start.16 = (bf16[384,512]{1,0:T(8,128)(2,1)S(1)}, bf16[384,512]{1,0:T(8,128)(2,1)}, u32[]{:S(2)}) copy-start(bf16[384,512]{1,0:T(8,128)(2,1)} %get-tuple-element.24) | copy-start | bytes 1179652
  674.0 3.4 copy-start.4
  674.0 6.2 copy-start.14
  679.2 0.9 copy-start.12
  794.0 3.4 copy-start.25
  794.0 5.3 copy-start.15
  956.9 3.6 copy-start.10
  956.9 3.6 copy-start.11
  963.7 3.8 copy-start.1
  963.7 3.8 copy-start.17
  963.7 3.8 copy-start.18
  965.6 12.4 %copy-start.5 = (f32[512,512]{0,1:T(8,128)}, f32[512,512]{0,1:T(8,128)S(1)}, u32[]{:S(2)}) copy-start(f32[512,512]{0,1:T(8,128)S(1)} %fusion.32) | copy-start | bytes 3145732
  967.5 4.9 copy-start.7
  969.5 1.0 copy-start.8
  972.4 5.6 copy-start.6
  982.9 5.3 copy-start.9
  982.9 5.3 copy-start.21
  982.9 5.3 copy-start.22
  992.5 2.4 copy-start.2
  992.5 2.5 copy-start.19
  992.5 2.8 copy-start.20
Sparse Core Ops, SparseCore 0:
  10.8 62.7 all-gather.7
  75.7 58.6 all-gather.3
  136.7 58.6 all-gather.5
  198.3 92.7 all-reduce.6
  313.6 118.1 reduce-scatter.6
  435.2 117.2 reduce-scatter.8
  556.7 117.2 reduce-scatter.10
  676.5 36.9 reduce-scatter.16
  716.1 37.7 reduce-scatter.12
  756.2 37.7 reduce-scatter.14
  800.5 156.3 all-reduce.4
where the time goes:
time: 1020 us; the launch traced here: 1010 us
  waiting for transfers between devices  754 us (74%)
  matrix products  177 us (17%)
  other arithmetic  32.6 us (3%)
  local copies, waits for them, and re-layouts  28.1 us (3%)
  between operations  14.5 us (1%)
    reduce_scatter x3, waiting for transfers between devices, local(): lax.psum_scatter(matmul(ancestor_inverse, lower_cols), 'col', scatter_dim...  236 us
    all_gather x3, waiting for transfers between devices, local(): lower_rows = lax.all_gather(lower_part, 'col', axis=0, tiled=True)  177 us
    psum x1, waiting for transfers between devices, local(): summed = lax.psum(left_dot(lower_here, stacked), ('row', 'col'))  147 us
    reduce_scatter x3, waiting for transfers between devices, local(): lax.psum_scatter(left_dot(ancestor_inverse, rows_float), 'row', scatter_d...  99.9 us
    dot_general x14, matrix products, matmul(): return jnp.dot(left, right, precision=highest)  96.3 us
    psum x1, waiting for transfers between devices, broadcast(): return lax.psum(kept, axis)  92.8 us
    dot_general x9, matrix products, left_dot(): lax.dot_general(left, right, (((0,), (0,)), ((), ())), precision=highest)  80.7 us
  transfers between devices with their start and end apart: 11, of which 11 were waited for; matrix products, arithmetic and copies ran while one was open for 15% of the time, Pallas kernels for 0%

commit v1 on v0

--- a/solution.py
+++ b/solution.py
@@ -8,7 +8,7 @@
 
 def broadcast(value, axis, source):
     kept = jnp.where(lax.axis_index(axis) == source, value, 0).astype(value.dtype)
-    return lax.psum(kept, axis)
+    return jnp.sum(lax.all_gather(kept, axis), axis=0)
 
 
 def matmul(left, right):

time: 1020 us -> 1040 us (1.020)
  waiting for transfers between devices: 754 us -> 771 us
  other arithmetic: 32.6 us -> 47.2 us
    psum x1 -> x0, waiting for transfers between devices: 92.8 us -> none  [broadcast(): return lax.psum(kept, axis)]
    all_gather x0 -> x3, waiting for transfers between devices: none -> 86.7 us  [broadcast(): return jnp.sum(lax.all_gather(kept, axis), axis=0)]
    reduce_scatter x3, waiting for transfers between devices: 236 us -> 259 us  [local(): lax.psum_scatter(matmul(ancestor_inverse, lower_cols), 'col', scatter_dim...]
    reduce_sum x0 -> x3, other arithmetic: none -> 14.5 us  [broadcast(): return jnp.sum(lax.all_gather(kept, axis), axis=0)]
  transfers between devices with their start and end apart: 11 -> 13, of which waited for: 11 -> 13; matrix products, arithmetic and copies ran while one was open for 15% -> 19% of each run, Pallas kernels for 0% -> 0%
where the time goes in v1:
time: 1040 us
  waiting for transfers between devices  771 us (74%)
  matrix products  177 us (17%)
  other arithmetic  47.2 us (5%)
  local copies, waits for them, and re-layouts  25.3 us (2%)
  between operations  14.7 us (1%)
    reduce_scatter x3, waiting for transfers between devices, local(): lax.psum_scatter(matmul(ancestor_inverse, lower_cols), 'col', scatter_dim...  259 us
    all_gather x3, waiting for transfers between devices, local(): lower_rows = lax.all_gather(lower_part, 'col', axis=0, tiled=True)  177 us
    psum x1, waiting for transfers between devices, local(): summed = lax.psum(left_dot(lower_here, stacked), ('row', 'col'))  146 us
    reduce_scatter x3, waiting for transfers between devices, local(): lax.psum_scatter(left_dot(ancestor_inverse, rows_float), 'row', scatter_d...  100 us
    dot_general x14, matrix products, matmul(): return jnp.dot(left, right, precision=highest)  95.9 us
    all_gather x3, waiting for transfers between devices, broadcast(): return jnp.sum(lax.all_gather(kept, axis), axis=0)  86.7 us
    dot_general x9, matrix products, left_dot(): lax.dot_general(left, right, (((0,), (0,)), ((), ())), precision=highest)  80.9 us
  transfers between devices with their start and end apart: 13, of which 13 were waited for; matrix products, arithmetic and copies ran while one was open for 19% of the time, Pallas kernels for 0%

profile of v1, /device:TPU:0, one launch (start us, length us, event | category | flops | bytes accessed | tf_op | source)
XLA Modules:
  0.0 1036.9 jit_solution(1162040543523967988)
XLA Ops:
  7.2 0.8 slice_bitcast_fusion.2
  8.1 2.5 bitcast_select_fusion.1
  12.2 61.3 %all-gather.10.cloned.1.call-done = bf16[3072,512]{1,0:T(8,128)(2,1)} async-done(((bf16[384,512]{1,0:T(8,128)(2,1)}), bf16[3072,512]{1,0:T(8,128)(2,1)}) %all-gather.10.cloned.1.call-update) | async-done | bytes 3145744 | tf_op jit(solution)/shard_map/all_gather | solution.py:43
  73.5 2.8 dynamic-slice_select_fusion.2
  76.4 58.0 %all-gather.12.cloned.1.call-done = bf16[3072,512]{1,0:T(8,128)(2,1)} async-done(((bf16[384,512]{1,0:T(8,128)(2,1)}), bf16[3072,512]{1,0:T(8,128)(2,1)}) %all-gather.12.cloned.1.call-update) | async-done | bytes 3145744 | tf_op jit(solution)/shard_map/all_gather | solution.py:43
  134.4 2.8 dynamic-slice_select_fusion.1
  137.3 58.0 %all-gather.14.cloned.1.call-done = bf16[3072,512]{1,0:T(8,128)(2,1)} async-done(((bf16[384,512]{1,0:T(8,128)(2,1)}), bf16[3072,512]{1,0:T(8,128)(2,1)}) %all-gather.14.cloned.1.call-update) | async-done | bytes 3145744 | tf_op jit(solution)/shard_map/all_gather | solution.py:43
  195.3 2.8 dynamic-slice_select_fusion
  198.2 44.2 %all-gather.16.cloned.1.call-done = bf16[6144,512]{1,0:T(8,128)(2,1)} async-done(((bf16[1536,512]{1,0:T(8,128)(2,1)}), bf16[6144,512]{1,0:T(8,128)(2,1)}) %all-gather.16.cloned.1.call-update) | async-done | bytes 6291472 | tf_op jit(solution)/shard_map/all_gather | solution.py:11
  242.4 4.8 reduce_sum.36
  247.2 21.9 %convolution_bitcast_fusion.2 = f32[3072,512]{0,1:T(8,128)} fusion(bf16[1536,512]{1,0:T(8,128)(2,1)S(1)} %reduce_sum.36, f32[3072,1536]{1,0:T(8,128)} %param.5), kind=kOutput, calls=%fused_computation.3 | convolution fusion | flops 28991029248 | bytes 26738688 | tf_op jit(solution)/shard_map/dot_general | solution.py:15
  269.7 21.1 %all-gather.18.cloned.1.call-done = bf16[6144,512]{1,0:T(8,128)(2,1)} async-done(((bf16[1536,512]{1,0:T(8,128)(2,1)}), bf16[6144,512]{1,0:T(8,128)(2,1)}) %all-gather.18.cloned.1.call-update) | async-done | bytes 6291472 | tf_op jit(solution)/shard_map/all_gather | solution.py:11
  290.8 4.8 reduce_sum.37
  295.6 21.9 %convolution_bitcast_fusion.1 = f32[3072,512]{0,1:T(8,128)} fusion(bf16[1536,512]{1,0:T(8,128)(2,1)S(1)} %reduce_sum.37, f32[3072,1536]{1,0:T(8,128)} %param.5), kind=kOutput, calls=%fused_computation.2 | convolution fusion | flops 28991029248 | bytes 26738688 | tf_op jit(solution)/shard_map/dot_general | solution.py:15
  317.7 21.4 %all-gather.20.cloned.1.call-done = bf16[6144,512]{1,0:T(8,128)(2,1)} async-done(((bf16[1536,512]{1,0:T(8,128)(2,1)}), bf16[6144,512]{1,0:T(8,128)(2,1)}) %all-gather.20.cloned.1.call-update) | async-done | bytes 6291472 | tf_op jit(solution)/shard_map/all_gather | solution.py:11
  339.1 4.8 reduce_sum.38
  344.0 21.8 %convolution_bitcast_fusion = f32[3072,512]{0,1:T(8,128)} fusion(bf16[1536,512]{1,0:T(8,128)(2,1)S(1)} %reduce_sum.38, f32[3072,1536]{1,0:T(8,128)} %param.5), kind=kOutput, calls=%fused_computation.1 | convolution fusion | flops 28991029248 | bytes 26738688 | tf_op jit(solution)/shard_map/dot_general | solution.py:15
  366.0 1.7 copy-done.28
  367.7 19.7 %convolution_bitcast_fusion.3 = f32[1536,512]{0,1:T(8,128)} fusion(bf16[3072,512]{1,0:T(8,128)(2,1)S(1)} %copy-done.28, f32[3072,1536]{1,0:T(8,128)} %param.5), kind=kOutput, calls=%fused_computation.4 | convolution fusion | flops 28991029248 | bytes 25165824 | tf_op jit(solution)/shard_map/dot_general | solution.py:19
  387.5 1.8 copy-done.27
  389.4 19.7 %convolution_bitcast_fusion.5 = f32[1536,512]{0,1:T(8,128)} fusion(bf16[3072,512]{1,0:T(8,128)(2,1)S(1)} %copy-done.27, f32[3072,1536]{1,0:T(8,128)} %param.5), kind=kOutput, calls=%fused_computation.6 | convolution fusion | flops 28991029248 | bytes 25165824 | tf_op jit(solution)/shard_map/dot_general | solution.py:19
  409.6 1.5 copy-done.26
  411.0 19.9 %convolution_bitcast_fusion.4 = f32[1536,512]{0,1:T(8,128)} fusion(bf16[3072,512]{1,0:T(8,128)(2,1)S(1)} %copy-done.26, f32[3072,1536]{1,0:T(8,128)} %param.5), kind=kOutput, calls=%fused_computation.5 | convolution fusion | flops 28991029248 | bytes 25165824 | tf_op jit(solution)/shard_map/dot_general | solution.py:19
  431.1 29.7 %reduce-scatter.7.cloned.1.call-done = f32[384,512]{0,1:T(8,128)} async-done(((f32[3072,512]{0,1:T(8,128)}), f32[384,512]{0,1:T(8,128)}) %reduce-scatter.7.cloned.1.call-update) | async-done | bytes 786448 | tf_op jit(solution)/shard_map/reduce_scatter | solution.py:47
  460.8 2.4 fusion.73
  463.2 3.2 fusion.64
  466.4 115.2 %reduce-scatter.9.cloned.1.call-done = f32[384,512]{0,1:T(8,128)} async-done(((f32[3072,512]{0,1:T(8,128)}), f32[384,512]{0,1:T(8,128)}) %reduce-scatter.9.cloned.1.call-update) | async-done | bytes 786448 | tf_op jit(solution)/shard_map/reduce_scatter | solution.py:47
  581.6 3.4 fusion.14
  585.0 0.9 copy-done.3
  585.9 3.1 fusion.6
  589.0 114.1 %reduce-scatter.11.cloned.1.call-done = f32[384,512]{0,1:T(8,128)} async-done(((f32[3072,512]{0,1:T(8,128)}), f32[384,512]{0,1:T(8,128)}) %reduce-scatter.11.cloned.1.call-update) | async-done | bytes 786448 | tf_op jit(solution)/shard_map/reduce_scatter | solution.py:47
  703.1 3.3 convolution_add_fusion.4
  706.5 1.9 fusion.15
  708.4 0.9 copy-done.12
  709.2 4.5 fusion
  713.8 2.3 slice.74
  716.1 2.7 copy.65
  718.8 23.7 %reduce-scatter.17.cloned.1.call-done = f32[384,512]{0,1:T(8,128)} async-done(((f32[1536,512]{0,1:T(8,128)}), f32[384,512]{0,1:T(8,128)}) %reduce-scatter.17.cloned.1.call-update) | async-done | bytes 786448 | tf_op jit(solution)/shard_map/reduce_scatter | solution.py:76
  742.5 40.3 %reduce-scatter.13.cloned.1.call-done = f32[384,512]{0,1:T(8,128)} async-done(((f32[1536,512]{0,1:T(8,128)}), f32[384,512]{0,1:T(8,128)}) %reduce-scatter.13.cloned.1.call-update) | async-done | bytes 786448 | tf_op jit(solution)/shard_map/reduce_scatter | solution.py:76
  782.8 4.1 convolution_add_fusion.1
  786.9 36.0 %reduce-scatter.15.cloned.1.call-done = f32[384,512]{0,1:T(8,128)} async-done(((f32[1536,512]{0,1:T(8,128)}), f32[384,512]{0,1:T(8,128)}) %reduce-scatter.15.cloned.1.call-update) | async-done | bytes 786448 | tf_op jit(solution)/shard_map/reduce_scatter | solution.py:76
  823.0 3.4 fusion.16
  826.4 1.9 fusion.18
  828.3 1.6 pad_maximum_fusion.2
  829.9 3.0 copy.51
  833.0 3.2 pad_maximum_fusion.1
  836.1 3.2 copy.50
  839.4 146.4 %all-reduce.3.cloned.1.call-done = (f32[512,1536]{1,0:T(8,128)}, f32[512,512]{1,0:T(8,128)}, f32[512,1024]{0,1:T(8,128)}) async-done(((f32[512,1536]{1,0:T(8,128)}, f32[512,512]{1,0:T(8,128)}, f32[512,1024]{0,1:T(8,128)}), (f32[512,1536]{1,0:T(8,128)}, f32[512,512]{1,0:T(8,128)}, f32[512,1024]{0,1:T(8,128)})) %all-reduce.3.cloned.1.call-update) | async-done | bytes 6291472 | tf_op jit(solution)/shard_map/psum | solution.py:56
  985.8 3.6 fusion.34
  989.4 3.2 bitcast_subtract_fusion.7
  992.6 1.9 fusion.32
  994.5 1.9 fusion.27
  996.5 2.0 fusion.13
  998.4 1.1 copy-done.8
  999.5 1.9 fusion.25
  1001.4 3.3 fusion.12
  1004.7 2.4 fusion.20
  1007.1 2.4 fusion.70
  1009.5 2.6 copy.39
  1012.0 5.3 fusion.11
  1017.4 2.0 maximum_bitcast_fusion.1
  1019.4 2.4 copy.49
  1021.8 2.3 maximum_bitcast_fusion.2
  1024.9 5.1 pad_maximum_fusion
  (82 shorter events, 4.4 us)
Async XLA Ops:
  7.2 66.4 %all-gather.10.cloned.1.call-start = ((), (), s32[]{:S(2)}) async-start(), calls=%async_computation.6 | async-start | bytes 3538944 | tf_op jit(solution)/shard_map/all_gather | solution.py:43
  10.7 123.8 %all-gather.12.cloned.1.call-start = ((), (), s32[]{:S(2)}) async-start(), calls=%async_computation.8 | async-start | bytes 3538944 | tf_op jit(solution)/shard_map/all_gather | solution.py:43
  11.4 183.9 %all-gather.14.cloned.1.call-start = ((), (), s32[]{:S(2)}) async-start(), calls=%async_computation.10 | async-start | bytes 3538944 | tf_op jit(solution)/shard_map/all_gather | solution.py:43
  12.1 230.2 %all-gather.16.cloned.1.call-start = ((), (), s32[]{:S(2)}) async-start(), calls=%async_computation.15 | async-start | bytes 7864320 | tf_op jit(solution)/shard_map/all_gather | solution.py:11
  76.4 214.4 %all-gather.18.cloned.1.call-start = ((), (), s32[]{:S(2)}) async-start(), calls=%async_computation.16 | async-start | bytes 7864320 | tf_op jit(solution)/shard_map/all_gather | solution.py:11
  137.3 201.9 %all-gather.20.cloned.1.call-start = ((), (), s32[]{:S(2)}) async-start(), calls=%async_computation.17 | async-start | bytes 7864320 | tf_op jit(solution)/shard_map/all_gather | solution.py:11
  198.2 262.6 %reduce-scatter.7.cloned.1.call-start = ((), (), s32[]{:S(2)}) async-start(), calls=%async_computation.7 | async-start | bytes 7077888 | tf_op jit(solution)/shard_map/reduce_scatter | solution.py:47
  269.1 312.5 %reduce-scatter.9.cloned.1.call-start = ((), (), s32[]{:S(2)}) async-start(), calls=%async_computation.9 | async-start | bytes 7077888 | tf_op jit(solution)/shard_map/reduce_scatter | solution.py:47
  317.5 385.6 %reduce-scatter.11.cloned.1.call-start = ((), (), s32[]{:S(2)}) async-start(), calls=%async_computation.11 | async-start | bytes 7077888 | tf_op jit(solution)/shard_map/reduce_scatter | solution.py:47
  365.7 1.9 copy-start.28
  365.8 376.7 %reduce-scatter.17.cloned.1.call-start = ((), (), s32[]{:S(2)}) async-start(), calls=%async_computation.14 | async-start | bytes 3932160 | tf_op jit(solution)/shard_map/reduce_scatter | solution.py:76
  387.4 1.9 copy-start.27
  387.5 395.4 %reduce-scatter.13.cloned.1.call-start = ((), (), s32[]{:S(2)}) async-start(), calls=%async_computation.12 | async-start | bytes 3932160 | tf_op jit(solution)/shard_map/reduce_scatter | solution.py:76
  409.1 1.9 copy-start.26
  409.1 413.9 %reduce-scatter.15.cloned.1.call-start = ((), (), s32[]{:S(2)}) async-start(), calls=%async_computation.13 | async-start | bytes 3932160 | tf_op jit(solution)/shard_map/reduce_scatter | solution.py:76
  431.0 32.2 %copy-start.23 = (bf16[384,512]{1,0:T(8,128)(2,1)S(1)}, bf16[384,512]{1,0:T(8,128)(2,1)}, u32[]{:S(2)}) copy-start(bf16[384,512]{1,0:T(8,128)(2,1)} %get-tuple-element.20) | copy-start | bytes 1179652
  431.0 150.7 %copy-start = (f32[3,512,512]{2,1,0:T(8,128)S(1)}, f32[3,512,512]{2,1,0:T(8,128)}, u32[]{:S(2)}) copy-start(f32[3,512,512]{2,1,0:T(8,128)} %param.7) | copy-start | bytes 9437188
  431.0 554.8 %all-reduce.3.cloned.1.call-start = ((), (), s32[]{:S(2)}) async-start(), calls=%async_computation.18 | async-start | bytes 12582912 | tf_op jit(solution)/shard_map/psum | solution.py:56
  466.4 119.5 %copy-start.24 = (bf16[384,512]{1,0:T(8,128)(2,1)S(1)}, bf16[384,512]{1,0:T(8,128)(2,1)}, u32[]{:S(2)}) copy-start(bf16[384,512]{1,0:T(8,128)(2,1)} %get-tuple-element.19) | copy-start | bytes 1179652
  581.6 4.2 copy-start.13
  585.0 0.9 copy-start.3
  589.0 120.2 %copy-start.16 = (bf16[384,512]{1,0:T(8,128)(2,1)S(1)}, bf16[384,512]{1,0:T(8,128)(2,1)}, u32[]{:S(2)}) copy-start(bf16[384,512]{1,0:T(8,128)(2,1)} %get-tuple-element.21) | copy-start | bytes 1179652
  703.1 3.4 copy-start.4
  703.1 6.1 copy-start.14
  708.4 0.9 copy-start.12
  823.0 3.4 copy-start.25
  823.0 5.3 copy-start.15
  985.8 3.6 copy-start.10
  985.8 3.6 copy-start.11
  992.6 3.8 copy-start.1
  992.6 3.8 copy-start.17
  992.6 3.8 copy-start.18
  994.5 12.6 %copy-start.5 = (f32[512,512]{0,1:T(8,128)}, f32[512,512]{0,1:T(8,128)S(1)}, u32[]{:S(2)}) copy-start(f32[512,512]{0,1:T(8,128)S(1)} %fusion.32) | copy-start | bytes 3145732
  996.4 5.0 copy-start.7
  998.4 1.1 copy-start.8
  1001.4 5.7 copy-start.6
  1012.0 5.3 copy-start.9
  1012.0 5.3 copy-start.21
  1012.0 5.3 copy-start.22
  1021.7 2.4 copy-start.2
  1021.8 2.5 copy-start.19
  1021.8 2.8 copy-start.20
Sparse Core Ops, SparseCore 0:
  10.8 62.7 all-gather.9
  75.7 58.6 all-gather.11
  136.6 58.6 all-gather.13
  197.3 45.0 all-gather.15
  244.4 46.3 all-gather.17
  292.8 46.3 all-gather.19
  342.7 117.9 reduce-scatter.6
  464.3 117.2 reduce-scatter.8
  585.8 117.2 reduce-scatter.10
  705.5 36.9 reduce-scatter.16
  745.1 37.7 reduce-scatter.12
  785.2 37.7 reduce-scatter.14
  829.5 156.2 all-reduce.2
